TPU v7x, 256 devices: a whole 4x4x8 slice. The times are simulated.
256 devices in a mesh: tok: 8 (over z), tp: 16 (over y, x), grp: 2 (over core).
Axes of the slice: x: 4, y: 4, z: 8, core: 2. Of those that a mesh axis runs over, the one named last changes fastest.
Arguments:
- hidden: bfloat16 [2048, 6144], P(('tok', 'grp'), 'tp'), may hold values from -6 to 6
- gain: bfloat16 [6144], P('tp'), may hold values from 0.5 to 1.5
- expert_ids: int32 [2048, 2], P(('tok', 'grp')), may hold values from 0 to 7, all different within a row; in each aligned block of 128 rows (0 to 127, 128 to 255, ...) at most 40 rows name the same one
- gate_weights: float32 [2048, 2], P(('tok', 'grp')), may hold values from 0.1 to 0.9
- segment_ids: int32 [2048], P(('tok', 'grp')), may hold values from 0 to 15, never falling along the last dimension, each value on 1 to 384 neighbouring positions
- upstream: bfloat16 [2048, 6144], P(('tok', 'grp'), 'tp'), may hold values from -6 to 6
- w_gate: bfloat16 [8, 6144, 8192], P('tok', None, ('tp', 'grp')), may hold values from -0.078125 to 0.078125
- w_up: bfloat16 [8, 6144, 8192], P('tok', None, ('tp', 'grp')), may hold values from -0.078125 to 0.078125
- w_down: bfloat16 [8, 8192, 6144], P('tok', ('tp', 'grp')), may hold values from -0.0625 to 0.0625
Outputs:
- mixed: bfloat16 [2048, 6144], P(('tok', 'grp'), 'tp')
- importance: float32 [8, 8192], P('tok', ('tp', 'grp'))
Inputs may be any that keep to these rules, and one draw needn't show every extreme that they name: `expert_ids`: each token names 2 different experts. Within the tokens of one token shard (aligned blocks of 128 rows) no expert is named by more than 40 tokens, and in some block one expert is named by exactly 40. `segment_ids`: never falling along the tokens; every document holds between 1 and 384 tokens.
All inputs are finite; a program needn't handle non-finite values.
Results may differ from a plain program's by a relative error of at most 0.0095.
Values may be sent and summed in bfloat16 or wider, within the bound.
No kernel may reach another device: no remote copies, remote signals or barrier semaphores. Data moves between devices by JAX's collectives and lax.ppermute only.
A program may use at most 128 MiB of HBM per device.

v0:
```python
import jax
import jax.numpy as jnp
from jax import lax
from jax.sharding import PartitionSpec as P


def expert_pass(rows_in, cot_in, gate_mat, up_mat, down_mat):
    gate_pre = jnp.dot(rows_in, gate_mat, preferred_element_type=jnp.float32)
    up_proj = jnp.dot(rows_in, up_mat, preferred_element_type=jnp.float32)
    sigmoid_gate = jax.nn.sigmoid(gate_pre)
    activated = gate_pre * sigmoid_gate
    hidden_act = (activated * up_proj).astype(jnp.bfloat16)
    grad_act = lax.dot_general(
        cot_in, down_mat, (((1,), (1,)), ((), ())), preferred_element_type=jnp.float32
    )
    grad_gate = (
        grad_act * up_proj * sigmoid_gate * (1.0 + gate_pre * (1.0 - sigmoid_gate))
    ).astype(jnp.bfloat16)
    grad_up = (grad_act * activated).astype(jnp.bfloat16)
    grad_wgate = lax.dot_general(
        rows_in, grad_gate, (((0,), (0,)), ((), ())), preferred_element_type=jnp.float32
    )
    grad_wup = lax.dot_general(
        rows_in, grad_up, (((0,), (0,)), ((), ())), preferred_element_type=jnp.float32
    )
    grad_wdown = lax.dot_general(
        hidden_act, cot_in, (((0,), (0,)), ((), ())), preferred_element_type=jnp.float32
    )
    scores = jnp.sum(jnp.abs(grad_wgate * gate_mat.astype(jnp.float32)), axis=0)
    scores = scores + jnp.sum(jnp.abs(grad_wup * up_mat.astype(jnp.float32)), axis=0)
    scores = scores + jnp.sum(jnp.abs(grad_wdown * down_mat.astype(jnp.float32)), axis=1)
    return (hidden_act, scores)


def on_device(hidden, gain, expert_ids, gate_weights, segment_ids, upstream, w_gate, w_up, w_down):
    rows_here = hidden.shape[0]
    top_count = expert_ids.shape[1]
    experts = lax.axis_size("tok")
    groups = lax.axis_size("grp")
    capacity = 5 * rows_here // (2 * experts)
    width = w_gate.shape[1]
    documents = jnp.arange(experts * groups, dtype=jnp.int32)
    doc_onehot = (segment_ids[:, None] == documents[None, :]).astype(jnp.float32)
    doc_len = lax.psum(jnp.sum(doc_onehot, axis=0), ("tok", "grp"))
    tok_len = jnp.sum(doc_onehot * doc_len[None, :], axis=1)
    tok_weight = rows_here / tok_len
    onehot = (
        expert_ids.reshape(-1)[:, None] == jnp.arange(experts, dtype=jnp.int32)[None, :]
    ).astype(jnp.int32)
    before = jnp.cumsum(onehot, axis=0) - onehot
    slot_ids = jnp.sum(before * onehot, axis=1).reshape(rows_here, top_count)
    targets = expert_ids * capacity + slot_ids
    all_slots = jnp.arange(experts * capacity, dtype=jnp.int32)
    matches = all_slots[:, None, None] == targets[None, :, :]
    placing = jnp.any(matches, axis=2).astype(jnp.bfloat16)
    scaled = gate_weights * tok_weight[:, None]
    slot_scale = jnp.sum(jnp.where(matches, scaled[None, :, :], 0.0), axis=(1, 2))
    combining = jnp.sum(jnp.where(matches, gate_weights[None, :, :], 0.0), axis=2)
    wide_hidden = hidden.astype(jnp.float32)
    squares = lax.psum(jnp.sum(wide_hidden * wide_hidden, axis=1), "tp")
    scaling = lax.rsqrt(squares / width + 1e-05)
    normed = (wide_hidden * scaling[:, None] * gain.astype(jnp.float32)[None, :]).astype(
        jnp.bfloat16
    )
    block_rows = jnp.dot(placing, normed, preferred_element_type=jnp.float32).astype(jnp.bfloat16)
    block_cot = jnp.dot(placing, upstream, preferred_element_type=jnp.float32) * slot_scale[:, None]
    block_rows = block_rows.reshape(experts, capacity, -1)
    block_cot = block_cot.astype(jnp.bfloat16).reshape(experts, capacity, -1)
    came_rows, came_cot = (
        lax.all_to_all(block_rows, "tok", split_axis=0, concat_axis=0, tiled=True),
        lax.all_to_all(block_cot, "tok", split_axis=0, concat_axis=0, tiled=True),
    )
    part_rows, part_cot = (
        lax.all_gather(came_rows, "tp", axis=2, tiled=True),
        lax.all_gather(came_cot, "tp", axis=2, tiled=True),
    )
    pooled_rows, pooled_cot = (
        lax.all_gather(part_rows, "grp", axis=0, tiled=True),
        lax.all_gather(part_cot, "grp", axis=0, tiled=True),
    )
    rows_in = pooled_rows.reshape(-1, width)
    cot_in = pooled_cot.reshape(-1, width)
    gate_mat = w_gate[0]
    up_mat = w_up[0]
    down_mat = w_down[0]
    hidden_act, scores = expert_pass(rows_in, cot_in, gate_mat, up_mat, down_mat)
    importance = scores / (rows_here * experts * groups)
    partial_value = lax.psum_scatter(
        lax.dot_general(
            down_mat, hidden_act, (((0,), (1,)), ((), ())), preferred_element_type=jnp.float32
        ).astype(jnp.bfloat16),
        "tp",
        scatter_dimension=0,
        tiled=True,
    )
    summed = lax.psum_scatter(partial_value, "grp", scatter_dimension=1, tiled=True).astype(
        jnp.float32
    )
    slice_width = summed.shape[0]
    outgoing = summed.astype(jnp.bfloat16).reshape(slice_width, experts, capacity)
    returned = lax.all_to_all(outgoing, "tok", split_axis=1, concat_axis=1, tiled=True)
    returned = returned.reshape(slice_width, experts * capacity).astype(jnp.float32)
    combined = lax.dot_general(
        combining,
        returned,
        (((0,), (1,)), ((), ())),
        precision=lax.Precision.HIGHEST,
        preferred_element_type=jnp.float32,
    )
    mixed = (hidden.astype(jnp.float32) + combined).astype(jnp.bfloat16)
    return (mixed, importance[None, :])


def solution(mesh):
    placed = (
        P(("tok", "grp"), "tp"),
        P("tp"),
        P(("tok", "grp"), None),
        P(("tok", "grp"), None),
        P(("tok", "grp")),
        P(("tok", "grp"), "tp"),
        P("tok", None, ("tp", "grp")),
        P("tok", None, ("tp", "grp")),
        P("tok", ("tp", "grp"), None),
    )
    return jax.shard_map(
        on_device,
        mesh=mesh,
        in_specs=placed,
        out_specs=(P(("tok", "grp"), "tp"), P("tok", ("tp", "grp"))),
        check_vma=False,
    )
```

profile of v0, /device:TPU:1, one launch (start us, length us, event | category | flops | bytes accessed | tf_op | source)
XLA Modules:
  0.0 378.7 jit_solution(2218602018310981666)
XLA Ops:
  7.2 0.0 copy-start
  7.2 0.0 copy-start.4
  7.2 0.0 all-gather.5.cloned.1.call-start
  7.2 0.9 copy.31
  8.2 0.1 eq.56
  8.3 0.1 eq.52
  8.5 1.0 fusion.19
  9.5 34.2 %psum.14 = f32[128]{0:T(128)S(1)} all-reduce(f32[128]{0:T(128)S(1)} %fusion.19), channel_id=1, replica_groups=mesh['tok'=8,'tp'=16,'grp'=2] {'tp'}, use_global_device_ids=true, to_apply=%region_6.7 | all-reduce | flops 128 | bytes 1024 | tf_op jit(solution)/shard_map/psum | solution.py:60
  43.7 0.7 convert_element_type.60
  44.4 0.6 reduce-window.6
  45.0 0.2 slice_reduce_fusion
  45.2 0.1 fusion.27
  45.3 0.1 reshape.79
  45.5 0.1 copy.33
  45.5 0.7 multiply_add_fusion
  46.3 1.2 convolution_convert_fusion.1
  47.5 17.2 %all_to_all.15 = bf16[8,40,384]{2,1,0:T(8,128)(2,1)} all-to-all(bf16[8,40,384]{2,1,0:T(8,128)(2,1)S(1)} %bitcast.56), channel_id=1, replica_groups=mesh['tok'=8,'tp'=16,'grp'=2] {'tok'}, dimensions={0} | all-to-all | bytes 491520 | tf_op jit(solution)/shard_map/all_to_all | solution.py:70
  64.7 0.0 all-gather.5.cloned.1.call-update
  64.7 0.0 all-gather.9.cloned.1.call-start
  64.8 0.8 convert_reduce_fusion
  65.6 32.2 %psum.15 = f32[16]{0:T(128)S(1)} all-reduce(f32[16]{0:T(128)S(1)} %convert_reduce_fusion), channel_id=1, replica_groups=mesh['tok'=8,'tp'=16,'grp'=2] {'tok','grp'}, use_global_device_ids=true, to_apply=%region_10.11 | all-reduce | flops 16 | bytes 128 | tf_op jit(solution)/shard_map/psum | solution.py:44
  97.8 0.7 select_reduce_fusion.2
  98.5 0.7 broadcast_multiply_fusion
  99.2 1.5 select_reduce_fusion
  100.7 0.0 copy-done
  100.7 0.2 fusion.14
  101.0 12.8 %all_to_all.16 = bf16[8,40,384]{2,1,0:T(8,128)(2,1)} all-to-all(bf16[8,40,384]{2,1,0:T(8,128)(2,1)S(1)} %bitcast.57), channel_id=1, replica_groups=mesh['tok'=8,'tp'=16,'grp'=2] {'tok'}, dimensions={0} | all-to-all | bytes 491520 | tf_op jit(solution)/shard_map/all_to_all | solution.py:71
  113.7 0.0 all-gather.9.cloned.1.call-update
  113.8 0.0 all-gather.7.cloned.1.call-start
  113.8 10.2 %all-gather.5.cloned.1.call-done = bf16[8,40,6144]{2,1,0:T(8,128)(2,1)} async-done(((bf16[8,40,384]{2,1,0:T(8,128)(2,1)}), bf16[8,40,6144]{2,1,0:T(8,128)(2,1)}) %all-gather.5.cloned.1.call-update) | async-done | bytes 3932176 | tf_op jit(solution)/shard_map/all_gather | solution.py:74
  124.0 0.0 all-gather.7.cloned.1.call-update
  124.1 0.0 all-gather.11.cloned.1.call-start
  124.1 62.4 %all-gather.9.cloned.1.call-done = bf16[8,40,6144]{2,1,0:T(8,128)(2,1)} async-done(((bf16[8,40,384]{2,1,0:T(8,128)(2,1)}), bf16[8,40,6144]{2,1,0:T(8,128)(2,1)}) %all-gather.9.cloned.1.call-update) | async-done | bytes 3932176 | tf_op jit(solution)/shard_map/all_gather | solution.py:75
  186.5 0.0 all-gather.11.cloned.1.call-update
  186.5 0.0 reduce-scatter.7.cloned.1.call-start
  186.5 27.7 %all-gather.7.cloned.1.call-done = bf16[16,40,6144]{2,1,0:T(8,128)(2,1)} async-done(((bf16[8,40,6144]{2,1,0:T(8,128)(2,1)}), bf16[16,40,6144]{2,1,0:T(8,128)(2,1)}) %all-gather.7.cloned.1.call-update) | async-done | bytes 7864336 | tf_op jit(solution)/shard_map/all_gather | solution.py:78
  214.2 0.0 copy-done.4
  214.2 5.6 %fusion.9 = f32[640,256]{1,0:T(8,128)S(1)} fusion(bf16[640,6144]{1,0:T(8,128)(2,1)} %bitcast.60, bf16[1,6144,256]{2,1,0:T(8,128)(2,1)S(1)} %copy-done.4), kind=kOutput, calls=%fused_computation.13 | convolution fusion | flops 2013265920 | bytes 11665408 | tf_op jit(solution)/shard_map/dot_general | solution.py:8
  219.8 0.0 copy-done.3
  219.8 0.8 copy-done.6
  220.6 3.0 multiply_convert_fusion.2
  223.6 0.0 copy-done.7
  223.6 0.7 copy-done.2
  224.4 0.0 copy-done.1
  224.4 6.1 %fusion = bf16[6144,640]{0,1:T(8,128)(2,1)} fusion(bf16[640,256]{1,0:T(8,128)(2,1)S(1)} %get-tuple-element.4, bf16[1,256,6144]{2,1,0:T(8,128)(2,1)S(1)} %copy-done.1), kind=kOutput, calls=%fused_computation.1 | convolution fusion | flops 2017198080 | bytes 11337728 | tf_op jit(solution)/shard_map/dot_general | solution.py:89
  230.5 10.7 %copy.34 = bf16[6144,640]{1,0:T(8,128)(2,1)} copy(bf16[6144,640]{0,1:T(8,128)(2,1)} %fusion) | data formatting | bytes 15728640
  241.2 0.0 reduce-scatter.7.cloned.1.call-update
  241.2 0.2 reduce-scatter.5.cloned.1.call-start
  241.5 0.1 all-gather.11.cloned.1.call-done
  241.6 5.6 %fusion.4 = f32[640,256]{1,0:T(8,128)S(1)} fusion(bf16[640,6144]{1,0:T(8,128)(2,1)} %bitcast.53, bf16[1,256,6144]{2,1,0:T(8,128)(2,1)S(1)} %copy-done.1), kind=kOutput, calls=%fused_computation.8 | convolution fusion | flops 2013265920 | bytes 11665408 | tf_op jit(solution)/shard_map/dot_general | solution.py:13
  247.2 0.0 copy-start.9
  247.2 0.8 copy-done.9
  248.1 0.0 copy-done.5
  248.1 6.2 %fusion.11 = f32[256]{0:T(256)S(1)} fusion(bf16[1,6144,256]{2,1,0:T(8,128)(2,1)S(1)} %copy-done.5, bf16[640,6144]{1,0:T(8,128)(2,1)} %bitcast.61, f32[640,256]{1,0:T(8,128)S(1)} %copy-done.8, f32[640,256]{1,0:T(8,128)S(1)} %fusion.4, f32[640,256]{1,0:T(8,128)S(1)} %copy-done.10), kind=kOutput, calls=%fused_computation.15 | convolution fusion | flops 2021195520 | bytes 12977152 | tf_op jit(solution)/shard_map/dot_general | solution.py:20
  254.3 80.1 %reduce-scatter.7.cloned.1.call-done = bf16[384,640]{1,0:T(8,128)(2,1)} async-done(((bf16[6144,640]{1,0:T(8,128)(2,1)}), bf16[384,640]{1,0:T(8,128)(2,1)}) %reduce-scatter.7.cloned.1.call-update) | async-done | bytes 491536
  334.4 2.0 copy.35
  336.4 0.0 reduce-scatter.5.cloned.1.call-update
  336.5 7.4 %fusion.12 = f32[256]{0:T(256)S(1)} fusion(bf16[1,6144,256]{2,1,0:T(8,128)(2,1)} %param.16, bf16[640,6144]{1,0:T(8,128)(2,1)} %bitcast.62, f32[640,256]{1,0:T(8,128)} %copy-done.9, f32[640,256]{1,0:T(8,128)} %copy-done.7), kind=kOutput, calls=%fused_computation.16 | convolution fusion | flops 2020540160 | bytes 12321792 | tf_op jit(solution)/shard_map/dot_general | solution.py:23
  343.8 7.7 %reduce-scatter.5.cloned.1.call-done = bf16[384,320]{0,1:T(8,128)(2,1)} async-done(((bf16[384,640]{0,1:T(8,128)(2,1)}), bf16[384,320]{0,1:T(8,128)(2,1)}) %reduce-scatter.5.cloned.1.call-update) | async-done | bytes 245776 | tf_op jit(solution)/shard_map/reduce_scatter | solution.py:96
  351.5 6.5 %all-to-all-start.1 = ((bf16[384,8,40]{0,2,1:T(8,128)(2,1)}), bf16[384,8,40]{0,2,1:T(8,128)(2,1)S(1)}, u32[]{:S(2)}, u32[]{:S(2)}) async-start(bf16[384,8,40]{0,2,1:T(8,128)(2,1)} %bitcast.58), calls=%async_computation.2 | async-start | bytes 491520 | tf_op jit(solution)/shard_map/all_to_all | solution.py:101
  358.0 6.5 %fusion.13 = f32[256]{0:T(256)S(1)} fusion(bf16[1,256,6144]{2,1,0:T(8,128)(2,1)S(1)} %copy-done.1, bf16[640,256]{1,0:T(8,128)(2,1)} %copy-done.2, bf16[640,6144]{1,0:T(8,128)(2,1)} %bitcast.54), kind=kOutput, calls=%fused_computation.17 | convolution fusion | flops 2019557120 | bytes 11338752 | tf_op jit(solution)/shard_map/dot_general | solution.py:26
  364.5 0.6 add_multiply_fusion
  365.0 4.8 %all-to-all-done.1 = bf16[384,8,40]{0,2,1:T(8,128)(2,1)S(1)} async-done(((bf16[384,8,40]{0,2,1:T(8,128)(2,1)}), bf16[384,8,40]{0,2,1:T(8,128)(2,1)S(1)}, u32[]{:S(2)}, u32[]{:S(2)}) %all-to-all-start.1) | async-done | bytes 245792 | tf_op jit(solution)/shard_map/all_to_all | solution.py:101
  369.8 2.0 fusion.15
  (16 shorter events, 0.1 us)
Async XLA Ops:
  7.2 93.6 %copy-start = (bf16[128,384]{1,0:T(8,128)(2,1)S(1)}, bf16[128,384]{1,0:T(8,128)(2,1)}, u32[]{:S(2)}) copy-start(bf16[128,384]{1,0:T(8,128)(2,1)} %param.14) | copy-start | bytes 294916
  7.2 207.0 %copy-start.4 = (bf16[1,6144,256]{2,1,0:T(8,128)(2,1)S(1)}, bf16[1,6144,256]{2,1,0:T(8,128)(2,1)}, u32[]{:S(2)}) copy-start(bf16[1,6144,256]{2,1,0:T(8,128)(2,1)} %param.15) | copy-start | bytes 9437188
  7.2 116.8 %all-gather.5.cloned.1.call-start = ((), (), s32[]{:S(2)}) async-start(), calls=%async_computation.5 | async-start | bytes 4177920 | tf_op jit(solution)/shard_map/all_gather | solution.py:74
  64.7 121.7 %all-gather.9.cloned.1.call-start = ((), (), s32[]{:S(2)}) async-start(), calls=%async_computation.8 | async-start | bytes 4177920 | tf_op jit(solution)/shard_map/all_gather | solution.py:75
  113.8 100.4 %all-gather.7.cloned.1.call-start = ((), (), s32[]{:S(2)}) async-start(), calls=%async_computation.6 | async-start | bytes 11796480 | tf_op jit(solution)/shard_map/all_gather | solution.py:78
  124.1 117.6 %all-gather.11.cloned.1.call-start = ((), (), s32[]{:S(2)}) async-start(), calls=%async_computation.9 | async-start | bytes 11796480 | tf_op jit(solution)/shard_map/all_gather | solution.py:79
  186.5 147.9 %reduce-scatter.7.cloned.1.call-start = ((), (), s32[]{:S(2)}) async-start(), calls=%async_computation.10 | async-start | bytes 8355840
  214.2 5.6 %copy-start.3 = (bf16[16,40,6144]{2,1,0:T(8,128)(2,1)S(1)}, bf16[16,40,6144]{2,1,0:T(8,128)(2,1)}, u32[]{:S(2)}) copy-start(bf16[16,40,6144]{2,1,0:T(8,128)(2,1)} %all-gather.7.cloned.1.call-done) | copy-start | bytes 23592964
  214.2 6.4 %copy-start.6 = (bf16[1,6144,256]{2,1,0:T(8,128)(2,1)S(1)}, bf16[1,6144,256]{2,1,0:T(8,128)(2,1)}, u32[]{:S(2)}) copy-start(bf16[1,6144,256]{2,1,0:T(8,128)(2,1)} %param.16) | copy-start | bytes 9437188
  220.6 3.0 copy-start.7
  220.6 3.8 copy-start.1
  223.6 0.7 copy-start.2
  241.2 110.2 %reduce-scatter.5.cloned.1.call-start = ((), (), s32[]{:S(2)}) async-start(), calls=%async_computation.7 | async-start | bytes 737280 | tf_op jit(solution)/shard_map/reduce_scatter | solution.py:96
  241.6 6.5 %copy-start.5 = (bf16[1,6144,256]{2,1,0:T(8,128)(2,1)S(1)}, bf16[1,6144,256]{2,1,0:T(8,128)(2,1)}, u32[]{:S(2)}) copy-start(bf16[1,6144,256]{2,1,0:T(8,128)(2,1)} %param.15) | copy-start | bytes 9437188
  241.6 6.5 %copy-start.8 = (f32[640,256]{1,0:T(8,128)S(1)}, f32[640,256]{1,0:T(8,128)}, u32[]{:S(2)}) copy-start(f32[640,256]{1,0:T(8,128)} %copy-done.7) | copy-start | bytes 1966084
  241.6 6.5 %copy-start.10 = (f32[640,256]{1,0:T(8,128)S(1)}, f32[640,256]{1,0:T(8,128)}, u32[]{:S(2)}) copy-start(f32[640,256]{1,0:T(8,128)} %get-tuple-element.5) | copy-start | bytes 1966084
  247.2 0.8 copy-start.9
  351.5 18.3 %all-to-all-start.1 = ((bf16[384,8,40]{0,2,1:T(8,128)(2,1)}), bf16[384,8,40]{0,2,1:T(8,128)(2,1)S(1)}, u32[]{:S(2)}, u32[]{:S(2)}) async-start(bf16[384,8,40]{0,2,1:T(8,128)(2,1)} %bitcast.58), calls=%async_computation.2 | async-start | bytes 491520 | tf_op jit(solution)/shard_map/all_to_all | solution.py:101
Sparse Core Ops, SparseCore 0:
  64.9 59.1 all-gather.4
  126.4 59.9 all-gather.8
  188.3 25.9 all-gather.6
  215.9 25.6 all-gather.10
  245.3 89.1 reduce-scatter.6
  336.8 14.6 reduce-scatter.4
where the time goes:
time: 379 us
  waiting for transfers between devices  193 us (51%)
  blocking collectives  96.5 us (25%)
  matrix products  43.9 us (12%)
  local copies, waits for them, and re-layouts  16.8 us (4%)
  between operations  14.2 us (4%)
  other arithmetic  7.42 us (2%)
  starting transfers between devices  6.89 us (2%)
    unnamed x7, waiting for transfers between devices  80.2 us
    all_gather x1, waiting for transfers between devices, on_device(): lax.all_gather(came_cot, 'tp', axis=2, tiled=True)  62.4 us
    psum x1, blocking collectives, on_device(): squares = lax.psum(jnp.sum(wide_hidden * wide_hidden, axis=1), 'tp')  34.2 us
    psum x1, blocking collectives, on_device(): doc_len = lax.psum(jnp.sum(doc_onehot, axis=0), ('tok', 'grp'))  32.2 us
    all_gather x1, waiting for transfers between devices, on_device(): lax.all_gather(part_rows, 'grp', axis=0, tiled=True)  27.7 us
    all_to_all x1, blocking collectives, on_device(): lax.all_to_all(block_rows, 'tok', split_axis=0, concat_axis=0, tiled=True)  17.2 us
    unnamed x25, local copies, waits for them, and re-layouts  16.1 us
    all_to_all x1, blocking collectives, on_device(): lax.all_to_all(block_cot, 'tok', split_axis=0, concat_axis=0, tiled=True)  12.8 us
  transfers between devices with their start and end apart: 7, of which 7 were waited for; matrix products, arithmetic and copies ran while one was open for 15% of the time, Pallas kernels for 0%

commit v1 on v0

--- a/solution.py
+++ b/solution.py
@@ -57,7 +57,9 @@
     slot_scale = jnp.sum(jnp.where(matches, scaled[None, :, :], 0.0), axis=(1, 2))
     combining = jnp.sum(jnp.where(matches, gate_weights[None, :, :], 0.0), axis=2)
     wide_hidden = hidden.astype(jnp.float32)
-    squares = lax.psum(jnp.sum(wide_hidden * wide_hidden, axis=1), "tp")
+    vec = jnp.sum(wide_hidden * wide_hidden, axis=1)
+    new = lax.all_gather(vec, "tp")
+    squares = jnp.sum(new, axis=0)
     scaling = lax.rsqrt(squares / width + 1e-05)
     normed = (wide_hidden * scaling[:, None] * gain.astype(jnp.float32)[None, :]).astype(
         jnp.bfloat16

time: 379 us -> 363 us (0.958)
  blocking collectives: 96.5 us -> 79.3 us
    psum x1 -> x0, blocking collectives: 34.2 us -> none  [on_device(): squares = lax.psum(jnp.sum(wide_hidden * wide_hidden, axis=1), 'tp')]
    all_gather x0 -> x1, blocking collectives: none -> 17.2 us  [on_device(): new = lax.all_gather(vec, 'tp')]
where the time goes in v1:
time: 363 us
  waiting for transfers between devices  194 us (53%)
  blocking collectives  79.3 us (22%)
  matrix products  43.9 us (12%)
  local copies, waits for them, and re-layouts  16.8 us (5%)
  between operations  14.2 us (4%)
  other arithmetic  7.48 us (2%)
  starting transfers between devices  6.89 us (2%)
    unnamed x7, waiting for transfers between devices  80.4 us
    all_gather x1, waiting for transfers between devices, on_device(): lax.all_gather(came_cot, 'tp', axis=2, tiled=True)  62.4 us
    psum x1, blocking collectives, on_device(): doc_len = lax.psum(jnp.sum(doc_onehot, axis=0), ('tok', 'grp'))  29.9 us
    all_gather x1, waiting for transfers between devices, on_device(): lax.all_gather(part_rows, 'grp', axis=0, tiled=True)  27.7 us
    all_to_all x1, blocking collectives, on_device(): lax.all_to_all(block_rows, 'tok', split_axis=0, concat_axis=0, tiled=True)  17.2 us
    all_gather x1, blocking collectives, on_device(): new = lax.all_gather(vec, 'tp')  17.2 us
    unnamed x25, local copies, waits for them, and re-layouts  16.1 us
    all_to_all x1, blocking collectives, on_device(): lax.all_to_all(block_cot, 'tok', split_axis=0, concat_axis=0, tiled=True)  15 us
  transfers between devices with their start and end apart: 7, of which 7 were waited for; matrix products, arithmetic and copies ran while one was open for 15% of the time, Pallas kernels for 0%

profile of v1, /device:TPU:1, one launch (start us, length us, event | category | flops | bytes accessed | tf_op | source)
XLA Modules:
  0.0 362.6 jit_solution(11167888134111405013)
XLA Ops:
  7.2 0.0 copy-start
  7.2 0.0 copy-start.4
  7.2 0.0 all-gather.7.cloned.1.call-start
  7.2 0.9 copy.31
  8.2 0.1 eq.56
  8.3 0.1 eq.52
  8.5 1.0 fusion.19
  9.5 0.7 convert_element_type.60
  10.2 17.2 %all-gather.1 = f32[16,1,128]{2,1,0:T(1,128)S(1)} all-gather(f32[1,1,128]{2,1,0:T(1,128)S(1)} %bitcast.60), channel_id=2, replica_groups=mesh['tok'=8,'tp'=16,'grp'=2] {'tp'}, dimensions={0}, use_global_device_ids=true | all-gather | bytes 8704 | tf_op jit(solution)/shard_map/all_gather | solution.py:61
  27.4 0.6 reduce-window.6
  27.9 0.2 slice_reduce_fusion
  28.2 0.1 fusion.27
  28.3 0.1 reshape.83
  28.4 0.1 copy.33
  28.5 0.7 multiply_add_fusion
  29.3 1.2 convolution_convert_fusion.1
  30.4 17.2 %all_to_all.15 = bf16[8,40,384]{2,1,0:T(8,128)(2,1)} all-to-all(bf16[8,40,384]{2,1,0:T(8,128)(2,1)S(1)} %bitcast.57), channel_id=1, replica_groups=mesh['tok'=8,'tp'=16,'grp'=2] {'tok'}, dimensions={0} | all-to-all | bytes 491520 | tf_op jit(solution)/shard_map/all_to_all | solution.py:72
  47.7 0.0 all-gather.7.cloned.1.call-update
  47.7 0.0 all-gather.11.cloned.1.call-start
  47.8 0.8 convert_reduce_fusion
  48.5 29.9 %psum.7 = f32[16]{0:T(128)S(1)} all-reduce(f32[16]{0:T(128)S(1)} %convert_reduce_fusion), channel_id=1, replica_groups=mesh['tok'=8,'tp'=16,'grp'=2] {'tok','grp'}, use_global_device_ids=true, to_apply=%region_10.11 | all-reduce | flops 16 | bytes 128 | tf_op jit(solution)/shard_map/psum | solution.py:44
  78.5 0.7 select_reduce_fusion.2
  79.2 0.7 broadcast_multiply_fusion
  79.9 1.5 select_reduce_fusion
  81.4 0.0 copy-done
  81.4 0.2 fusion.14
  81.6 15.0 %all_to_all.16 = bf16[8,40,384]{2,1,0:T(8,128)(2,1)} all-to-all(bf16[8,40,384]{2,1,0:T(8,128)(2,1)S(1)} %bitcast.58), channel_id=1, replica_groups=mesh['tok'=8,'tp'=16,'grp'=2] {'tok'}, dimensions={0} | all-to-all | bytes 491520 | tf_op jit(solution)/shard_map/all_to_all | solution.py:73
  96.6 0.0 all-gather.11.cloned.1.call-update
  96.7 0.0 all-gather.9.cloned.1.call-start
  96.7 11.0 %all-gather.7.cloned.1.call-done = bf16[8,40,6144]{2,1,0:T(8,128)(2,1)} async-done(((bf16[8,40,384]{2,1,0:T(8,128)(2,1)}), bf16[8,40,6144]{2,1,0:T(8,128)(2,1)}) %all-gather.7.cloned.1.call-update) | async-done | bytes 3932176 | tf_op jit(solution)/shard_map/all_gather | solution.py:76
  107.7 0.0 all-gather.9.cloned.1.call-update
  107.7 0.0 all-gather.13.cloned.1.call-start
  107.8 62.4 %all-gather.11.cloned.1.call-done = bf16[8,40,6144]{2,1,0:T(8,128)(2,1)} async-done(((bf16[8,40,384]{2,1,0:T(8,128)(2,1)}), bf16[8,40,6144]{2,1,0:T(8,128)(2,1)}) %all-gather.11.cloned.1.call-update) | async-done | bytes 3932176 | tf_op jit(solution)/shard_map/all_gather | solution.py:77
  170.1 0.0 all-gather.13.cloned.1.call-update
  170.1 0.0 reduce-scatter.7.cloned.1.call-start
  170.2 27.7 %all-gather.9.cloned.1.call-done = bf16[16,40,6144]{2,1,0:T(8,128)(2,1)} async-done(((bf16[8,40,6144]{2,1,0:T(8,128)(2,1)}), bf16[16,40,6144]{2,1,0:T(8,128)(2,1)}) %all-gather.9.cloned.1.call-update) | async-done | bytes 7864336 | tf_op jit(solution)/shard_map/all_gather | solution.py:80
  197.9 0.0 copy-done.4
  197.9 5.6 %fusion.9 = f32[640,256]{1,0:T(8,128)S(1)} fusion(bf16[640,6144]{1,0:T(8,128)(2,1)} %bitcast.62, bf16[1,6144,256]{2,1,0:T(8,128)(2,1)S(1)} %copy-done.4), kind=kOutput, calls=%fused_computation.13 | convolution fusion | flops 2013265920 | bytes 11665408 | tf_op jit(solution)/shard_map/dot_general | solution.py:8
  203.5 0.0 copy-done.3
  203.5 0.8 copy-done.6
  204.2 3.0 multiply_convert_fusion.2
  207.3 0.0 copy-done.7
  207.3 0.7 copy-done.2
  208.0 0.0 copy-done.1
  208.0 6.1 %fusion = bf16[6144,640]{0,1:T(8,128)(2,1)} fusion(bf16[640,256]{1,0:T(8,128)(2,1)S(1)} %get-tuple-element.4, bf16[1,256,6144]{2,1,0:T(8,128)(2,1)S(1)} %copy-done.1), kind=kOutput, calls=%fused_computation.1 | convolution fusion | flops 2017198080 | bytes 11337728 | tf_op jit(solution)/shard_map/dot_general | solution.py:91
  214.1 10.7 %copy.34 = bf16[6144,640]{1,0:T(8,128)(2,1)} copy(bf16[6144,640]{0,1:T(8,128)(2,1)} %fusion) | data formatting | bytes 15728640
  224.9 0.0 reduce-scatter.7.cloned.1.call-update
  224.9 0.2 reduce-scatter.5.cloned.1.call-start
  225.1 0.1 all-gather.13.cloned.1.call-done
  225.3 5.6 %fusion.4 = f32[640,256]{1,0:T(8,128)S(1)} fusion(bf16[640,6144]{1,0:T(8,128)(2,1)} %bitcast.54, bf16[1,256,6144]{2,1,0:T(8,128)(2,1)S(1)} %copy-done.1), kind=kOutput, calls=%fused_computation.8 | convolution fusion | flops 2013265920 | bytes 11665408 | tf_op jit(solution)/shard_map/dot_general | solution.py:13
  230.9 0.0 copy-start.9
  230.9 0.8 copy-done.9
  231.7 0.0 copy-done.5
  231.7 6.2 %fusion.11 = f32[256]{0:T(256)S(1)} fusion(bf16[1,6144,256]{2,1,0:T(8,128)(2,1)S(1)} %copy-done.5, bf16[640,6144]{1,0:T(8,128)(2,1)} %bitcast.63, f32[640,256]{1,0:T(8,128)S(1)} %copy-done.8, f32[640,256]{1,0:T(8,128)S(1)} %fusion.4, f32[640,256]{1,0:T(8,128)S(1)} %copy-done.10), kind=kOutput, calls=%fused_computation.15 | convolution fusion | flops 2021195520 | bytes 12977152 | tf_op jit(solution)/shard_map/dot_general | solution.py:20
  238.0 80.3 %reduce-scatter.7.cloned.1.call-done = bf16[384,640]{1,0:T(8,128)(2,1)} async-done(((bf16[6144,640]{1,0:T(8,128)(2,1)}), bf16[384,640]{1,0:T(8,128)(2,1)}) %reduce-scatter.7.cloned.1.call-update) | async-done | bytes 491536
  318.2 2.0 copy.35
  320.3 0.0 reduce-scatter.5.cloned.1.call-update
  320.3 7.4 %fusion.12 = f32[256]{0:T(256)S(1)} fusion(bf16[1,6144,256]{2,1,0:T(8,128)(2,1)} %param.16, bf16[640,6144]{1,0:T(8,128)(2,1)} %bitcast.64, f32[640,256]{1,0:T(8,128)} %copy-done.9, f32[640,256]{1,0:T(8,128)} %copy-done.7), kind=kOutput, calls=%fused_computation.16 | convolution fusion | flops 2020540160 | bytes 12321792 | tf_op jit(solution)/shard_map/dot_general | solution.py:23
  327.6 7.7 %reduce-scatter.5.cloned.1.call-done = bf16[384,320]{0,1:T(8,128)(2,1)} async-done(((bf16[384,640]{0,1:T(8,128)(2,1)}), bf16[384,320]{0,1:T(8,128)(2,1)}) %reduce-scatter.5.cloned.1.call-update) | async-done | bytes 245776 | tf_op jit(solution)/shard_map/reduce_scatter | solution.py:98
  335.4 6.5 %all-to-all-start.1 = ((bf16[384,8,40]{0,2,1:T(8,128)(2,1)}), bf16[384,8,40]{0,2,1:T(8,128)(2,1)S(1)}, u32[]{:S(2)}, u32[]{:S(2)}) async-start(bf16[384,8,40]{0,2,1:T(8,128)(2,1)} %bitcast.59), calls=%async_computation.2 | async-start | bytes 491520 | tf_op jit(solution)/shard_map/all_to_all | solution.py:103
  341.8 6.5 %fusion.13 = f32[256]{0:T(256)S(1)} fusion(bf16[1,256,6144]{2,1,0:T(8,128)(2,1)S(1)} %copy-done.1, bf16[640,256]{1,0:T(8,128)(2,1)} %copy-done.2, bf16[640,6144]{1,0:T(8,128)(2,1)} %bitcast.55), kind=kOutput, calls=%fused_computation.17 | convolution fusion | flops 2019557120 | bytes 11338752 | tf_op jit(solution)/shard_map/dot_general | solution.py:26
  348.3 0.6 add_multiply_fusion
  348.9 4.8 %all-to-all-done.1 = bf16[384,8,40]{0,2,1:T(8,128)(2,1)S(1)} async-done(((bf16[384,8,40]{0,2,1:T(8,128)(2,1)}), bf16[384,8,40]{0,2,1:T(8,128)(2,1)S(1)}, u32[]{:S(2)}, u32[]{:S(2)}) %all-to-all-start.1) | async-done | bytes 245792 | tf_op jit(solution)/shard_map/all_to_all | solution.py:103
  353.7 2.0 fusion.15
  (17 shorter events, 0.2 us)
Async XLA Ops:
  7.2 74.2 %copy-start = (bf16[128,384]{1,0:T(8,128)(2,1)S(1)}, bf16[128,384]{1,0:T(8,128)(2,1)}, u32[]{:S(2)}) copy-start(bf16[128,384]{1,0:T(8,128)(2,1)} %param.14) | copy-start | bytes 294916
  7.2 190.7 %copy-start.4 = (bf16[1,6144,256]{2,1,0:T(8,128)(2,1)S(1)}, bf16[1,6144,256]{2,1,0:T(8,128)(2,1)}, u32[]{:S(2)}) copy-start(bf16[1,6144,256]{2,1,0:T(8,128)(2,1)} %param.15) | copy-start | bytes 9437188
  7.2 100.5 %all-gather.7.cloned.1.call-start = ((), (), s32[]{:S(2)}) async-start(), calls=%async_computation.5 | async-start | bytes 4177920 | tf_op jit(solution)/shard_map/all_gather | solution.py:76
  47.7 122.4 %all-gather.11.cloned.1.call-start = ((), (), s32[]{:S(2)}) async-start(), calls=%async_computation.8 | async-start | bytes 4177920 | tf_op jit(solution)/shard_map/all_gather | solution.py:77
  96.7 101.2 %all-gather.9.cloned.1.call-start = ((), (), s32[]{:S(2)}) async-start(), calls=%async_computation.6 | async-start | bytes 11796480 | tf_op jit(solution)/shard_map/all_gather | solution.py:80
  107.7 117.6 %all-gather.13.cloned.1.call-start = ((), (), s32[]{:S(2)}) async-start(), calls=%async_computation.9 | async-start | bytes 11796480 | tf_op jit(solution)/shard_map/all_gather | solution.py:81
  170.1 148.1 %reduce-scatter.7.cloned.1.call-start = ((), (), s32[]{:S(2)}) async-start(), calls=%async_computation.10 | async-start | bytes 8355840
  197.9 5.6 %copy-start.3 = (bf16[16,40,6144]{2,1,0:T(8,128)(2,1)S(1)}, bf16[16,40,6144]{2,1,0:T(8,128)(2,1)}, u32[]{:S(2)}) copy-start(bf16[16,40,6144]{2,1,0:T(8,128)(2,1)} %all-gather.9.cloned.1.call-done) | copy-start | bytes 23592964
  197.9 6.4 %copy-start.6 = (bf16[1,6144,256]{2,1,0:T(8,128)(2,1)S(1)}, bf16[1,6144,256]{2,1,0:T(8,128)(2,1)}, u32[]{:S(2)}) copy-start(bf16[1,6144,256]{2,1,0:T(8,128)(2,1)} %param.16) | copy-start | bytes 9437188
  204.2 3.0 copy-start.7
  204.2 3.8 %copy-start.1 = (bf16[1,256,6144]{2,1,0:T(8,128)(2,1)S(1)}, bf16[1,256,6144]{2,1,0:T(8,128)(2,1)}, u32[]{:S(2)}) copy-start(bf16[1,256,6144]{2,1,0:T(8,128)(2,1)} %param.17) | copy-start | bytes 9437188
  207.3 0.7 copy-start.2
  224.9 110.5 %reduce-scatter.5.cloned.1.call-start = ((), (), s32[]{:S(2)}) async-start(), calls=%async_computation.7 | async-start | bytes 737280 | tf_op jit(solution)/shard_map/reduce_scatter | solution.py:98
  225.3 6.5 %copy-start.5 = (bf16[1,6144,256]{2,1,0:T(8,128)(2,1)S(1)}, bf16[1,6144,256]{2,1,0:T(8,128)(2,1)}, u32[]{:S(2)}) copy-start(bf16[1,6144,256]{2,1,0:T(8,128)(2,1)} %param.15) | copy-start | bytes 9437188
  225.3 6.5 %copy-start.8 = (f32[640,256]{1,0:T(8,128)S(1)}, f32[640,256]{1,0:T(8,128)}, u32[]{:S(2)}) copy-start(f32[640,256]{1,0:T(8,128)} %copy-done.7) | copy-start | bytes 1966084
  225.3 6.5 %copy-start.10 = (f32[640,256]{1,0:T(8,128)S(1)}, f32[640,256]{1,0:T(8,128)}, u32[]{:S(2)}) copy-start(f32[640,256]{1,0:T(8,128)} %get-tuple-element.5) | copy-start | bytes 1966084
  230.9 0.8 copy-start.9
  335.4 18.3 %all-to-all-start.1 = ((bf16[384,8,40]{0,2,1:T(8,128)(2,1)}), bf16[384,8,40]{0,2,1:T(8,128)(2,1)S(1)}, u32[]{:S(2)}, u32[]{:S(2)}) async-start(bf16[384,8,40]{0,2,1:T(8,128)(2,1)} %bitcast.59), calls=%async_computation.2 | async-start | bytes 491520 | tf_op jit(solution)/shard_map/all_to_all | solution.py:103
Sparse Core Ops, SparseCore 0:
  47.8 59.8 all-gather.6
  110.1 59.9 all-gather.10
  171.9 25.9 all-gather.8
  199.5 25.6 all-gather.12
  228.9 89.2 reduce-scatter.6
  320.6 14.6 reduce-scatter.4
